TPU v7x, 512 devices: a whole 4x4x16 slice. The times are simulated.
512 devices in a mesh: row: 8 (over z_hi, core), col: 16 (over y, z_lo), depth: 4 (over x).
Axes of the slice: x: 4, y: 4, z: 16 (z_hi: 4, z_lo: 4; z = z_hi * 4 + z_lo), core: 2. Of those that a mesh axis runs over, the one named last changes fastest.
Arguments:
- values: bfloat16 [768, 16, 128, 128], P(('row', 'col')), may hold values from -0.47851562 to 0.47851562
- columns: int32 [768, 16], replicated, may hold values from 0 to 767, as said below
Outputs:
- purified: bfloat16 [768, 16, 128, 128], P(('row', 'col'), 'depth')
Inputs may be any that keep to these rules, and one draw needn't show every extreme that they name: Each block row a names 16 different block columns, a itself among them, all within 8 of a around the cycle of 768 block rows (indices wrap).
All inputs are finite; a program needn't handle non-finite values.
Results may differ from a plain program's by a relative error of at most 0.0047.
Values may be sent and summed in bfloat16 or wider, within the bound.
A program may use at most 128 MiB of HBM per device.

v0:
```python
import jax
import jax.numpy as jnp
from jax import lax
from jax.sharding import PartitionSpec as P

HB = 8


def passed_along(value, axis, by):
    peers = lax.axis_size(axis)
    return lax.ppermute(value, axis, [(i, (i + by) % peers) for i in range(peers)])


def matched_blocks(nearby, band_start, own_cols, target_cols, columns):
    total_blocks = columns.shape[0]
    band_count = nearby.shape[0]
    slot_count = nearby.shape[1]
    partner_cols = jnp.take(columns, own_cols, axis=0)
    same_column = partner_cols[:, :, None, :] == target_cols[:, None, :, None]
    slot_ids = jnp.arange(slot_count, dtype=jnp.int32)
    present = jnp.any(same_column, axis=3)
    chosen = jnp.sum(jnp.where(same_column, slot_ids, 0), axis=3)
    offset = jnp.mod(own_cols - band_start, total_blocks)
    inside = offset < band_count
    usable = inside[:, :, None] & present
    flat_index = jnp.where(
        usable, offset[:, :, None] * slot_count + chosen, band_count * slot_count
    )
    flat_blocks = nearby.reshape(band_count * slot_count, nearby.shape[2], nearby.shape[3])
    return jnp.take(flat_blocks, flat_index, axis=0, mode="fill", fill_value=0)


def local(values, columns):
    own_rows, slot_count, block_size, _ = values.shape
    layers = lax.axis_size("depth")
    quarter = slot_count // layers
    layer_index = lax.axis_index("depth")
    group_index = lax.axis_index(("row", "col"))
    first_row = group_index * own_rows
    own_cols = lax.dynamic_slice_in_dim(columns, first_row, own_rows, 0)
    target_cols = lax.dynamic_slice_in_dim(own_cols, layer_index * quarter, quarter, 1)
    hop_count = (HB + own_rows - 1) // own_rows
    reach_last = HB - (hop_count - 1) * own_rows
    lower_parts = []
    upper_parts = []
    for hop_step in range(1, hop_count + 1):
        edge_rows = own_rows if hop_step < hop_count else reach_last
        from_lower = passed_along(values[own_rows - edge_rows :], ("row", "col"), hop_step)
        from_upper = passed_along(values[:edge_rows], ("row", "col"), -hop_step)
        lower_parts.insert(0, from_lower)
        upper_parts.append(from_upper)
    below_rows = jnp.concatenate(lower_parts, axis=0)
    above_rows = jnp.concatenate(upper_parts, axis=0)
    nearby = jnp.concatenate([below_rows, values, above_rows], axis=0)
    selected = matched_blocks(nearby, first_row - HB, own_cols, target_cols, columns)
    square32 = jnp.einsum("aixy,aijyz->ajxz", values, selected, preferred_element_type=jnp.float32)
    square = square32.astype(jnp.bfloat16)
    whole_square = lax.all_gather(square, "depth", axis=1, tiled=True)
    cube32 = jnp.einsum(
        "aixy,aijyz->ajxz", whole_square, selected, preferred_element_type=jnp.float32
    )
    return (3.0 * square32 - 2.0 * cube32).astype(jnp.bfloat16)


def solution(mesh):
    placed = (P(("row", "col"), None, None, None), P())
    return jax.shard_map(
        local,
        mesh=mesh,
        in_specs=placed,
        out_specs=P(("row", "col"), "depth", None, None),
        check_vma=False,
    )
```

profile of v0, /device:TPU:1, one launch (start us, length us, event | category | flops | bytes accessed | tf_op | source)
XLA Modules:
  0.0 335.9 jit_solution(13076159911926167194)
XLA Ops:
  6.5 4.6 %collective-permute-start.1 = (bf16[6,16,128,128]{3,2,1,0:T(8,128)(2,1)}, bf16[6,16,128,128]{3,2,1,0:T(8,128)(2,1)}, u32[]{:S(2)}, u32[]{:S(2)}) collective-permute-start(bf16[6,16,128,128]{3,2,1,0:T(8,128)(2,1)} %param.2), channel_id=1, source_target_pairs={{0,4},{4,8},{8,12},{12,16},{16,20},{20,24},{24,28},{28,32},{32,36}... | collective-permute-start | bytes 9437192 | tf_op jit(solution)/shard_map/ppermute | solution.py:11
  11.2 7.6 %collective-permute-start.2 = (bf16[6,16,128,128]{3,2,1,0:T(8,128)(2,1)}, bf16[6,16,128,128]{3,2,1,0:T(8,128)(2,1)}, u32[]{:S(2)}, u32[]{:S(2)}) collective-permute-start(bf16[6,16,128,128]{3,2,1,0:T(8,128)(2,1)} %param.2), channel_id=1, source_target_pairs={{0,508},{4,0},{8,4},{12,8},{16,12},{20,16},{24,20},{28,24},{32,28}... | collective-permute-start | bytes 9437192 | tf_op jit(solution)/shard_map/ppermute | solution.py:11
  18.8 3.2 fusion.18
  22.0 1.9 collective-permute-start
  23.9 6.7 %collective-permute-start.3 = (bf16[2,16,128,128]{3,2,1,0:T(8,128)(2,1)}, bf16[2,16,128,128]{3,2,1,0:T(8,128)(2,1)}, u32[]{:S(2)}, u32[]{:S(2)}) collective-permute-start(bf16[2,16,128,128]{3,2,1,0:T(8,128)(2,1)} %get-tuple-element.7), channel_id=1, source_target_pairs={{0,504},{4,508},{8,0},{12,4},{16,8},{20,12},{24,16},{28,20},{32,24... | collective-permute-start | bytes 3145736 | tf_op jit(solution)/shard_map/ppermute | solution.py:11
  30.6 1.0 copy.39
  31.5 0.5 compare_and_fusion.1
  32.1 0.6 reshape.50
  32.7 0.7 pad_clamp_fusion.1
  33.3 1.4 dynamic_slice.7
  34.7 0.8 copy.41
  35.5 1.2 gather_fusion
  36.7 0.9 broadcast_select_fusion.7
  37.6 0.6 compare_reduce_fusion
  38.1 0.6 fusion.14
  38.7 0.1 copy.43
  38.9 0.1 reshape.58
  39.0 0.1 copy.42
  39.1 138.4 %collective-permute-done = bf16[2,16,128,128]{3,2,1,0:T(8,128)(2,1)} collective-permute-done((bf16[2,16,128,128]{3,2,1,0:T(8,128)(2,1)}, bf16[2,16,128,128]{3,2,1,0:T(8,128)(2,1)}, u32[]{:S(2)}, u32[]{:S(2)}) %collective-permute-start) | collective-permute-done | bytes 1048608 | tf_op jit(solution)/shard_map/ppermute | solution.py:11
  177.5 2.4 constant_dynamic-update-slice_fusion.4
  179.8 3.9 %constant_dynamic-update-slice_fusion.3 = bf16[22,16,128,128]{3,2,1,0:T(8,128)(2,1)} fusion(bf16[22,16,128,128]{3,2,1,0:T(8,128)(2,1)} %constant_dynamic-update-slice_fusion.4, bf16[6,16,128,128]{3,2,1,0:T(8,128)(2,1)} %collective-permute-done.1), kind=kLoop, calls=%fused_computation.30 | loop fusion | bytes 6291456
  183.8 2.1 constant_dynamic-update-slice_fusion.2
  185.9 4.0 %constant_dynamic-update-slice_fusion.1 = bf16[22,16,128,128]{3,2,1,0:T(8,128)(2,1)} fusion(bf16[22,16,128,128]{3,2,1,0:T(8,128)(2,1)} %constant_dynamic-update-slice_fusion.2, bf16[6,16,128,128]{3,2,1,0:T(8,128)(2,1)} %collective-permute-done.2), kind=kLoop, calls=%fused_computation.28 | loop fusion | bytes 6291456
  189.8 50.2 %collective-permute-done.3 = bf16[2,16,128,128]{3,2,1,0:T(8,128)(2,1)} collective-permute-done((bf16[2,16,128,128]{3,2,1,0:T(8,128)(2,1)}, bf16[2,16,128,128]{3,2,1,0:T(8,128)(2,1)}, u32[]{:S(2)}, u32[]{:S(2)}) %collective-permute-start.3) | collective-permute-done | bytes 1048608 | tf_op jit(solution)/shard_map/ppermute | solution.py:11
  240.1 2.3 constant_dynamic-update-slice_fusion
  242.4 15.5 %gather_fusion.1 = bf16[384,128,128]{2,1,0:T(8,128)(2,1)} fusion(bf16[352,128,128]{2,1,0:T(8,128)(2,1)} %bitcast.1, s32[1024]{0:T(1024)S(1)} %pad_clamp_fusion), kind=kCustom, calls=%fused_computation.1 | custom fusion | bytes 25167360 | tf_op jit(solution)/shard_map/jit(_take)/gather | solution.py:30
  257.9 7.9 %fusion = f32[6,4,128,128,1]{3,2,1,4,0:T(8,128)S(1)} fusion(bf16[6,16,4,128,128]{4,3,2,1,0:T(8,128)(2,1)} %bitcast.62, pred[6,16,4]{2,1,0:T(8,128)(4,1)S(1)} %copy.42, bf16[6,16,128,128]{3,2,1,0:T(8,128)(2,1)S(1)} %copy-done), kind=kOutput, calls=%fused_computation.3 | convolution fusion | flops 1616904192 | bytes 17301888 | tf_op jit(solution)/shard_map/aixy,aijyz->ajxz/dot_general | solution.py:56
  265.8 1.1 copy-done.1
  266.9 1.0 fusion.13
  268.0 51.1 %all-gather.2.cloned.1.call-done = bf16[6,16,128,128]{2,3,1,0:T(8,128)(2,1)} async-done(((bf16[6,4,128,128]{2,3,1,0:T(8,128)(2,1)}), bf16[6,16,128,128]{2,3,1,0:T(8,128)(2,1)}) %all-gather.2.cloned.1.call-update) | async-done | bytes 3145744 | tf_op jit(solution)/shard_map/all_gather | solution.py:58
  319.1 8.7 %fusion.10 = bf16[6,4,128,128]{2,3,1,0:T(8,128)(2,1)S(1)} fusion(bf16[6,16,128,128]{2,3,1,0:T(8,128)(2,1)} %all-gather.2.cloned.1.call-done, bf16[6,16,4,128,128]{4,3,2,1,0:T(8,128)(2,1)} %bitcast.63, pred[6,16,4]{2,1,0:T(8,128)(4,1)S(1)} %copy.42, f32[6,4,128,128,1]{3,2,1,4,0:T(8,128)} %copy-done.1), kind=kOutput, calls=%fused_computation.14 | convolution fusion | flops 1618477056 | bytes 18088320 | tf_op jit(solution)/shard_map/aixy,aijyz->ajxz/dot_general | solution.py:59
  327.9 1.2 copy.47
  (11 shorter events, 0.1 us)
Async XLA Ops:
  6.5 177.3 %copy-start = (bf16[6,16,128,128]{3,2,1,0:T(8,128)(2,1)S(1)}, bf16[6,16,128,128]{3,2,1,0:T(8,128)(2,1)}, u32[]{:S(2)}) copy-start(bf16[6,16,128,128]{3,2,1,0:T(8,128)(2,1)} %param.2) | copy-start | bytes 9437188
  6.5 312.6 %all-gather.2.cloned.1.call-start = ((), (), s32[]{:S(2)}) async-start(), calls=%async_computation | async-start | bytes 3932160 | tf_op jit(solution)/shard_map/all_gather | solution.py:58
  6.5 173.3 %collective-permute-start.1 = (bf16[6,16,128,128]{3,2,1,0:T(8,128)(2,1)}, bf16[6,16,128,128]{3,2,1,0:T(8,128)(2,1)}, u32[]{:S(2)}, u32[]{:S(2)}) collective-permute-start(bf16[6,16,128,128]{3,2,1,0:T(8,128)(2,1)} %param.2), channel_id=1, source_target_pairs={{0,4},{4,8},{8,12},{12,16},{16,20},{20,24},{24,28},{28,32},{32,36}... | collective-permute-start | bytes 9437192 | tf_op jit(solution)/shard_map/ppermute | solution.py:11
  11.2 174.7 %collective-permute-start.2 = (bf16[6,16,128,128]{3,2,1,0:T(8,128)(2,1)}, bf16[6,16,128,128]{3,2,1,0:T(8,128)(2,1)}, u32[]{:S(2)}, u32[]{:S(2)}) collective-permute-start(bf16[6,16,128,128]{3,2,1,0:T(8,128)(2,1)} %param.2), channel_id=1, source_target_pairs={{0,508},{4,0},{8,4},{12,8},{16,12},{20,16},{24,20},{28,24},{32,28}... | collective-permute-start | bytes 9437192 | tf_op jit(solution)/shard_map/ppermute | solution.py:11
  22.0 155.5 %collective-permute-start = (bf16[2,16,128,128]{3,2,1,0:T(8,128)(2,1)}, bf16[2,16,128,128]{3,2,1,0:T(8,128)(2,1)}, u32[]{:S(2)}, u32[]{:S(2)}) collective-permute-start(bf16[2,16,128,128]{3,2,1,0:T(8,128)(2,1)} %get-tuple-element.8), channel_id=1, source_target_pairs={{0,8},{4,12},{8,16},{12,20},{16,24},{20,28},{24,32},{28,36},{32,40... | collective-permute-start | bytes 3145736 | tf_op jit(solution)/shard_map/ppermute | solution.py:11
  23.9 216.2 %collective-permute-start.3 = (bf16[2,16,128,128]{3,2,1,0:T(8,128)(2,1)}, bf16[2,16,128,128]{3,2,1,0:T(8,128)(2,1)}, u32[]{:S(2)}, u32[]{:S(2)}) collective-permute-start(bf16[2,16,128,128]{3,2,1,0:T(8,128)(2,1)} %get-tuple-element.7), channel_id=1, source_target_pairs={{0,504},{4,508},{8,0},{12,4},{16,8},{20,12},{24,16},{28,20},{32,24... | collective-permute-start | bytes 3145736 | tf_op jit(solution)/shard_map/ppermute | solution.py:11
  265.8 1.1 copy-start.1
Sparse Core Ops, SparseCore 0:
  268.1 50.9 all-gather.1
where the time goes:
time: 336 us
  waiting for transfers between devices  240 us (71%)
  local copies, waits for them, and re-layouts  40.9 us (12%)
  starting transfers between devices  20.8 us (6%)
  matrix products  16.6 us (5%)
  between operations  13.5 us (4%)
  other arithmetic  4.28 us (1%)
    ppermute x4, waiting for transfers between devices, passed_along(): lax.ppermute(value, axis, [(i, (i + by) % peers) for i in range(peers)])  189 us
    all_gather x1, waiting for transfers between devices, local(): whole_square = lax.all_gather(square, 'depth', axis=1, tiled=True)  51.1 us
    ppermute x4, starting transfers between devices, passed_along(): lax.ppermute(value, axis, [(i, (i + by) % peers) for i in range(peers)])  20.8 us
    gather x1, local copies, waits for them, and re-layouts, matched_blocks(): return jnp.take(flat_blocks, flat_index, axis=0, mode='fill', fill_value=0)  15.5 us
    unnamed x9, local copies, waits for them, and re-layouts  14.4 us
    dot_general x1, matrix products, local(): jnp.einsum('aixy,aijyz->ajxz', whole_square, selected, preferred_element_...  8.72 us
    dot_general x1, matrix products, local(): jnp.einsum('aixy,aijyz->ajxz', values, selected, preferred_element_type=j...  7.87 us
  transfers between devices with their start and end apart: 5, of which 3 were waited for; matrix products, arithmetic and copies ran while one was open for 7% of the time, Pallas kernels for 0%

commit v1 on v0

--- a/solution.py
+++ b/solution.py
@@ -55,7 +55,9 @@
     selected = matched_blocks(nearby, first_row - HB, own_cols, target_cols, columns)
     square32 = jnp.einsum("aixy,aijyz->ajxz", values, selected, preferred_element_type=jnp.float32)
     square = square32.astype(jnp.bfloat16)
-    whole_square = lax.all_gather(square, "depth", axis=1, tiled=True)
+    whole_square = jnp.concatenate(
+        lax.all_to_all(jnp.stack([square] * lax.axis_size("depth")), "depth", 0, 0), axis=1
+    )
     cube32 = jnp.einsum(
         "aixy,aijyz->ajxz", whole_square, selected, preferred_element_type=jnp.float32
     )

time: 336 us -> 313 us (0.932)
  waiting for transfers between devices: 240 us -> 190 us
  blocking collectives: 0 us -> 40.4 us
  between operations: 13.5 us -> 0.17 us
    all_gather x1 -> x0, waiting for transfers between devices: 51.1 us -> none  [local(): whole_square = lax.all_gather(square, 'depth', axis=1, tiled=True)]
    all_to_all x0 -> x1, blocking collectives: none -> 40.4 us  [local(): lax.all_to_all(jnp.stack([square] * lax.axis_size('depth')), 'depth', 0, 0)]
    unnamed x9 -> x11, local copies, waits for them, and re-layouts: 14.4 us -> 14.5 us
  transfers between devices with their start and end apart: 5 -> 4, of which waited for: 3 -> 2; matrix products, arithmetic and copies ran while one was open for 7% -> 7% of each run, Pallas kernels for 0% -> 0%
where the time goes in v1:
time: 313 us; the launch traced here: 312 us
  waiting for transfers between devices  190 us (61%)
  local copies, waits for them, and re-layouts  41.9 us (13%)
  blocking collectives  40.4 us (13%)
  starting transfers between devices  20.8 us (7%)
  matrix products  15.9 us (5%)
    ppermute x4, waiting for transfers between devices, passed_along(): lax.ppermute(value, axis, [(i, (i + by) % peers) for i in range(peers)])  190 us
    all_to_all x1, blocking collectives, local(): lax.all_to_all(jnp.stack([square] * lax.axis_size('depth')), 'depth', 0, 0)  40.4 us
    ppermute x4, starting transfers between devices, passed_along(): lax.ppermute(value, axis, [(i, (i + by) % peers) for i in range(peers)])  20.8 us
    gather x1, local copies, waits for them, and re-layouts, matched_blocks(): return jnp.take(flat_blocks, flat_index, axis=0, mode='fill', fill_value=0)  15.5 us
    unnamed x11, local copies, waits for them, and re-layouts  14.5 us
    dot_general x1, matrix products, local(): jnp.einsum('aixy,aijyz->ajxz', whole_square, selected, preferred_element_...  7.99 us
    dot_general x1, matrix products, local(): jnp.einsum('aixy,aijyz->ajxz', values, selected, preferred_element_type=j...  7.87 us
  transfers between devices with their start and end apart: 4, of which 2 were waited for; matrix products, arithmetic and copies ran while one was open for 7% of the time, Pallas kernels for 0%

profile of v1, /device:TPU:1, one launch (start us, length us, event | category | flops | bytes accessed | tf_op | source)
XLA Modules:
  0.0 311.7 jit_solution(9051530413614695806)
XLA Ops:
  0.0 4.6 %collective-permute-start.1 = (bf16[6,16,128,128]{3,2,1,0:T(8,128)(2,1)}, bf16[6,16,128,128]{3,2,1,0:T(8,128)(2,1)}, u32[]{:S(2)}, u32[]{:S(2)}) collective-permute-start(bf16[6,16,128,128]{3,2,1,0:T(8,128)(2,1)} %param.2), channel_id=1, source_target_pairs={{0,4},{4,8},{8,12},{12,16},{16,20},{20,24},{24,28},{28,32},{32,36}... | collective-permute-start | bytes 9437192 | tf_op jit(solution)/shard_map/ppermute | solution.py:11
  4.6 7.6 %collective-permute-start.2 = (bf16[6,16,128,128]{3,2,1,0:T(8,128)(2,1)}, bf16[6,16,128,128]{3,2,1,0:T(8,128)(2,1)}, u32[]{:S(2)}, u32[]{:S(2)}) collective-permute-start(bf16[6,16,128,128]{3,2,1,0:T(8,128)(2,1)} %param.2), channel_id=1, source_target_pairs={{0,508},{4,0},{8,4},{12,8},{16,12},{20,16},{24,20},{28,24},{32,28}... | collective-permute-start | bytes 9437192 | tf_op jit(solution)/shard_map/ppermute | solution.py:11
  12.3 3.2 %fusion.13 = (bf16[2,16,128,128]{3,2,1,0:T(8,128)(2,1)}, bf16[2,16,128,128]{3,2,1,0:T(8,128)(2,1)}) fusion(bf16[6,16,128,128]{3,2,1,0:T(8,128)(2,1)} %param.2), kind=kLoop, calls=%fused_computation.40 | loop fusion | bytes 4194304 | tf_op jit(solution)/shard_map/slice | solution.py:49
  15.5 1.9 collective-permute-start
  17.4 6.7 %collective-permute-start.3 = (bf16[2,16,128,128]{3,2,1,0:T(8,128)(2,1)}, bf16[2,16,128,128]{3,2,1,0:T(8,128)(2,1)}, u32[]{:S(2)}, u32[]{:S(2)}) collective-permute-start(bf16[2,16,128,128]{3,2,1,0:T(8,128)(2,1)} %get-tuple-element.7), channel_id=1, source_target_pairs={{0,504},{4,508},{8,0},{12,4},{16,8},{20,12},{24,16},{28,20},{32,24... | collective-permute-start | bytes 3145736 | tf_op jit(solution)/shard_map/ppermute | solution.py:11
  24.0 1.0 copy.53
  25.0 0.6 compare_and_fusion.1
  25.7 1.4 dynamic_slice.7
  27.1 0.8 copy.55
  27.8 1.2 gather_fusion
  29.0 0.9 broadcast_select_fusion.7
  29.9 0.6 compare_reduce_fusion
  30.5 0.6 fusion.9
  31.1 0.1 copy.57
  31.3 0.1 copy.56
  31.5 139.5 %collective-permute-done = bf16[2,16,128,128]{3,2,1,0:T(8,128)(2,1)} collective-permute-done((bf16[2,16,128,128]{3,2,1,0:T(8,128)(2,1)}, bf16[2,16,128,128]{3,2,1,0:T(8,128)(2,1)}, u32[]{:S(2)}, u32[]{:S(2)}) %collective-permute-start) | collective-permute-done | bytes 1048608 | tf_op jit(solution)/shard_map/ppermute | solution.py:11
  170.9 2.4 constant_dynamic-update-slice_fusion.4
  173.3 3.9 %constant_dynamic-update-slice_fusion.3 = bf16[22,16,128,128]{3,2,1,0:T(8,128)(2,1)} fusion(bf16[22,16,128,128]{3,2,1,0:T(8,128)(2,1)} %constant_dynamic-update-slice_fusion.4, bf16[6,16,128,128]{3,2,1,0:T(8,128)(2,1)} %collective-permute-done.1), kind=kLoop, calls=%fused_computation.29 | loop fusion | bytes 6291456
  177.3 2.1 constant_dynamic-update-slice_fusion.2
  179.3 4.0 %constant_dynamic-update-slice_fusion.1 = bf16[22,16,128,128]{3,2,1,0:T(8,128)(2,1)} fusion(bf16[22,16,128,128]{3,2,1,0:T(8,128)(2,1)} %constant_dynamic-update-slice_fusion.2, bf16[6,16,128,128]{3,2,1,0:T(8,128)(2,1)} %collective-permute-done.2), kind=kLoop, calls=%fused_computation.27 | loop fusion | bytes 6291456
  183.3 50.3 %collective-permute-done.3 = bf16[2,16,128,128]{3,2,1,0:T(8,128)(2,1)} collective-permute-done((bf16[2,16,128,128]{3,2,1,0:T(8,128)(2,1)}, bf16[2,16,128,128]{3,2,1,0:T(8,128)(2,1)}, u32[]{:S(2)}, u32[]{:S(2)}) %collective-permute-start.3) | collective-permute-done | bytes 1048608 | tf_op jit(solution)/shard_map/ppermute | solution.py:11
  233.5 2.3 constant_dynamic-update-slice_fusion
  235.9 15.5 %gather_fusion.1 = bf16[384,128,128]{2,1,0:T(8,128)(2,1)} fusion(bf16[352,128,128]{2,1,0:T(8,128)(2,1)} %bitcast.1, s32[1024]{0:T(1024)S(1)} %pad_clamp_fusion), kind=kCustom, calls=%fused_computation.1 | custom fusion | bytes 25167360 | tf_op jit(solution)/shard_map/jit(_take)/gather | solution.py:30
  251.4 7.9 %fusion = f32[6,4,128,128,1]{3,2,1,4,0:T(8,128)S(1)} fusion(bf16[6,16,4,128,128]{4,3,2,1,0:T(8,128)(2,1)} %bitcast.61, pred[6,16,4]{2,1,0:T(8,128)(4,1)S(1)} %copy.56, bf16[6,16,128,128]{3,2,1,0:T(8,128)(2,1)S(1)} %copy-done), kind=kOutput, calls=%fused_computation.3 | convolution fusion | flops 1616904192 | bytes 17301888 | tf_op jit(solution)/shard_map/aixy,aijyz->ajxz/dot_general | solution.py:56
  259.3 1.2 copy-done.1
  260.5 0.1 fusion.8
  260.7 0.4 copy.59
  261.0 0.8 stack.2
  261.9 40.4 %all_to_all.5 = bf16[4,6,4,128,128]{4,3,2,1,0:T(8,128)(2,1)S(1)} all-to-all(bf16[4,6,4,128,128]{4,3,2,1,0:T(8,128)(2,1)S(1)} %stack.2), channel_id=1, replica_groups=mesh['row'=8,'col'=16,'depth'=4] {'depth'}, dimensions={0} | all-to-all | bytes 6291456 | tf_op jit(solution)/shard_map/all_to_all | solution.py:59
  302.3 0.2 copy.60
  302.5 8.0 %fusion.7 = bf16[6,4,128,128]{2,3,1,0:T(8,128)(2,1)S(1)} fusion(bf16[6,16,128,128,1]{3,2,4,1,0:T(8,128)(2,1)S(1)} %bitcast.63, bf16[6,16,4,128,128]{4,3,2,1,0:T(8,128)(2,1)} %bitcast.62, pred[6,16,4]{2,1,0:T(8,128)(4,1)S(1)} %copy.56, f32[6,4,128,128,1]{3,2,1,4,0:T(8,128)S(1)} %copy-done.2), kind=kOutput, calls=%fused_computation.13 | convolution fusion | flops 1618477056 | bytes 18088320 | tf_op jit(solution)/shard_map/aixy,aijyz->ajxz/dot_general | solution.py:61
  310.5 1.2 copy.62
  (14 shorter events, 0.3 us)
Async XLA Ops:
  0.0 177.2 %copy-start = (bf16[6,16,128,128]{3,2,1,0:T(8,128)(2,1)S(1)}, bf16[6,16,128,128]{3,2,1,0:T(8,128)(2,1)}, u32[]{:S(2)}) copy-start(bf16[6,16,128,128]{3,2,1,0:T(8,128)(2,1)} %param.2) | copy-start | bytes 9437188
  0.0 173.3 %collective-permute-start.1 = (bf16[6,16,128,128]{3,2,1,0:T(8,128)(2,1)}, bf16[6,16,128,128]{3,2,1,0:T(8,128)(2,1)}, u32[]{:S(2)}, u32[]{:S(2)}) collective-permute-start(bf16[6,16,128,128]{3,2,1,0:T(8,128)(2,1)} %param.2), channel_id=1, source_target_pairs={{0,4},{4,8},{8,12},{12,16},{16,20},{20,24},{24,28},{28,32},{32,36}... | collective-permute-start | bytes 9437192 | tf_op jit(solution)/shard_map/ppermute | solution.py:11
  4.6 174.7 %collective-permute-start.2 = (bf16[6,16,128,128]{3,2,1,0:T(8,128)(2,1)}, bf16[6,16,128,128]{3,2,1,0:T(8,128)(2,1)}, u32[]{:S(2)}, u32[]{:S(2)}) collective-permute-start(bf16[6,16,128,128]{3,2,1,0:T(8,128)(2,1)} %param.2), channel_id=1, source_target_pairs={{0,508},{4,0},{8,4},{12,8},{16,12},{20,16},{24,20},{28,24},{32,28}... | collective-permute-start | bytes 9437192 | tf_op jit(solution)/shard_map/ppermute | solution.py:11
  15.5 155.5 %collective-permute-start = (bf16[2,16,128,128]{3,2,1,0:T(8,128)(2,1)}, bf16[2,16,128,128]{3,2,1,0:T(8,128)(2,1)}, u32[]{:S(2)}, u32[]{:S(2)}) collective-permute-start(bf16[2,16,128,128]{3,2,1,0:T(8,128)(2,1)} %get-tuple-element.8), channel_id=1, source_target_pairs={{0,8},{4,12},{8,16},{12,20},{16,24},{20,28},{24,32},{28,36},{32,40... | collective-permute-start | bytes 3145736 | tf_op jit(solution)/shard_map/ppermute | solution.py:11
  17.4 216.2 %collective-permute-start.3 = (bf16[2,16,128,128]{3,2,1,0:T(8,128)(2,1)}, bf16[2,16,128,128]{3,2,1,0:T(8,128)(2,1)}, u32[]{:S(2)}, u32[]{:S(2)}) collective-permute-start(bf16[2,16,128,128]{3,2,1,0:T(8,128)(2,1)} %get-tuple-element.7), channel_id=1, source_target_pairs={{0,504},{4,508},{8,0},{12,4},{16,8},{20,12},{24,16},{28,20},{32,24... | collective-permute-start | bytes 3145736 | tf_op jit(solution)/shard_map/ppermute | solution.py:11
  259.3 1.2 copy-start.1
  260.6 41.8 %copy-start.2 = (f32[6,4,128,128,1]{3,2,1,4,0:T(8,128)S(1)}, f32[6,4,128,128,1]{3,2,1,4,0:T(8,128)}, u32[]{:S(2)}) copy-start(f32[6,4,128,128,1]{3,2,1,4,0:T(8,128)} %copy-done.1) | copy-start | bytes 4718596
